TPU v7x, 32 devices: a whole 2x2x4 slice. The times are simulated.
32 devices in a mesh: term: 4 (over y, x), sector: 8 (over z, core).
Axes of the slice: x: 2, y: 2, z: 4, core: 2. Of those that a mesh axis runs over, the one named last changes fastest.
Arguments:
- psi: bfloat16 [8, 8, 128, 128], P('sector'), may hold values from -6 to 6
- left_env: bfloat16 [8, 8, 128, 128], P('term', 'sector'), may hold values from -40 to 40
- right_env: bfloat16 [8, 8, 128, 128], P('term', 'sector'), may hold values from -4 to 4
- precond: bfloat16 [8, 8, 128, 128], P('sector'), may hold values from 0.5 to 4
- block_sizes: int32 [8], replicated, may hold values from 32 to 128, as said below
Outputs:
- state: bfloat16 [8, 8, 128, 128], P('sector')
- energy: float32 [3], replicated
Inputs may be any that keep to these rules, and one draw needn't show every extreme that they name: `block_sizes`: some sector has exactly 128 rows in every draw.
All inputs are finite; a program needn't handle non-finite values.
Results may differ from a plain program's by a relative error of at most 0.022.
Values may be sent and summed in bfloat16 or wider, within the bound.
No kernel may reach another device: no remote copies, remote signals or barrier semaphores. Data moves between devices by JAX's collectives and lax.ppermute only.
A program may use at most 128 MiB of HBM per device.

v0:
```python
import jax
import jax.numpy as jnp
from jax import lax
from jax.sharding import PartitionSpec as P

ITERS = 3


def block_mask(block_sizes, width, own_row):
    rows = jnp.arange(width)
    valid = rows[None, :] < block_sizes[:, None]
    own_valid = lax.dynamic_slice_in_dim(valid, own_row, 1, 0)[0]
    return (own_valid[None, :, None] & valid[:, None, :]).astype(jnp.float32)


def dot_sums(cur_share, img_share, pre_share, count):
    first = lax.psum(
        (jnp.sum(cur_share * cur_share), jnp.sum(cur_share * img_share)), ("term", "sector")
    )
    theta = first[1] / first[0]
    fresh = cur_share - (img_share - theta * cur_share) / pre_share
    squares = lax.psum(jnp.sum(fresh * fresh), ("term", "sector"))
    return (theta, lax.rsqrt(squares / count + 1e-06))


def local(psi, left_env, right_env, precond, block_sizes):
    sectors = block_sizes.shape[0]
    width = psi.shape[-1]
    own_row = lax.axis_index("sector")
    share = sectors // lax.axis_size("term")
    share_start = lax.axis_index("term") * share
    count = float(sectors * sectors * width * width)
    mask = block_mask(block_sizes, width, own_row)
    state = (psi[0].astype(jnp.float32) * mask).astype(jnp.bfloat16)
    scaling = precond[0].astype(jnp.float32)
    left_own = left_env[:, 0]

    def portion(values):
        return lax.dynamic_slice_in_dim(values, share_start, share, 0)

    right_all = lax.all_gather(right_env, "sector", axis=1, tiled=True)
    energies = []
    for step in range(ITERS):
        images = jnp.einsum(
            "jab,kjcb->kjac", state, right_all, preferred_element_type=jnp.float32
        ).astype(jnp.bfloat16)
        partial_value = jnp.einsum(
            "kac,kjcd->jad", left_own, images, preferred_element_type=jnp.float32
        )
        current = state.astype(jnp.float32)
        image = lax.psum(partial_value.astype(jnp.bfloat16), "term").astype(jnp.float32) * mask
        theta, factor = dot_sums(portion(current), portion(image), portion(scaling), count)
        fresh = current - (image - theta * current) / scaling
        state = (fresh * factor).astype(jnp.bfloat16)
        energies.append(theta)
    return (state[None], jnp.stack(energies))


def solution(mesh):
    in_specs = (
        P("sector", None, None, None),
        P("term", "sector", None, None),
        P("term", "sector", None, None),
        P("sector", None, None, None),
        P(),
    )
    out_specs = (P("sector", None, None, None), P())
    return jax.shard_map(local, mesh=mesh, in_specs=in_specs, out_specs=out_specs, check_vma=False)
```

profile of v0, /device:TPU:0, one launch (start us, length us, event | category | flops | bytes accessed | tf_op | source)
XLA Modules:
  0.0 424.9 jit_solution(16946019127858269423)
XLA Ops:
  7.2 0.6 copy-done.6
  8.0 1.1 copy.7
  9.1 16.6 %all_gather.3 = bf16[2,8,128,128]{3,2,1,0:T(8,128)(2,1)S(1)} all-gather(bf16[2,1,128,128]{3,2,1,0:T(8,128)(2,1)S(1)} %copy-done.5), channel_id=1, replica_groups=mesh['term'=4,'sector'=8] {'sector'}, dimensions={1}, use_global_device_ids=true | all-gather | bytes 589824 | tf_op jit(solution)/shard_map/all_gather | solution.py:41
  25.7 1.2 fusion.8
  27.1 0.9 copy-done.4
  28.1 43.0 %all-reduce.7.cloned.1.call-done = bf16[8,128,128]{1,2,0:T(8,128)(2,1)} async-done(((bf16[8,128,128]{1,2,0:T(8,128)(2,1)}), bf16[8,128,128]{1,2,0:T(8,128)(2,1)}) %all-reduce.7.cloned.1.call-update) | async-done | bytes 262160 | tf_op jit(solution)/shard_map/psum | solution.py:51
  71.1 1.2 fusion.34
  72.3 0.6 multiply_reduce_fusion.4
  72.9 39.6 %all-reduce.2 = (f32[]{:T(128)}, f32[]{:T(128)}) all-reduce(f32[]{:T(128)} %get-tuple-element.9, f32[]{:T(128)} %get-tuple-element.8), channel_id=1, replica_groups=mesh['term'=4,'sector'=8] {'term','sector'}, use_global_device_ids=true, to_apply=%region_2.0 | all-reduce | flops 2 | bytes 16 | tf_op jit(solution)/shard_map/psum | solution.py:17
  113.9 0.7 fusion.43
  114.5 41.4 %psum.87 = f32[]{:T(128)} all-reduce(f32[]{:T(128)} %fusion.43), channel_id=1, replica_groups=mesh['term'=4,'sector'=8] {'term','sector'}, use_global_device_ids=true, to_apply=%region_6.0 | all-reduce | flops 1 | bytes 8 | tf_op jit(solution)/shard_map/psum | solution.py:22
  156.9 1.2 fusion.7
  158.1 43.0 %all-reduce.9.cloned.1.call-done = bf16[8,128,128]{1,2,0:T(8,128)(2,1)} async-done(((bf16[8,128,128]{1,2,0:T(8,128)(2,1)}), bf16[8,128,128]{1,2,0:T(8,128)(2,1)}) %all-reduce.9.cloned.1.call-update) | async-done | bytes 262160 | tf_op jit(solution)/shard_map/psum | solution.py:51
  201.2 1.1 and_select_fusion.1
  203.0 39.6 %all-reduce.1 = (f32[]{:T(128)}, f32[]{:T(128)}) all-reduce(f32[]{:T(128)} %get-tuple-element.7, f32[]{:T(128)} %get-tuple-element.6), channel_id=1, replica_groups=mesh['term'=4,'sector'=8] {'term','sector'}, use_global_device_ids=true, to_apply=%region_9.0 | all-reduce | flops 2 | bytes 16 | tf_op jit(solution)/shard_map/psum | solution.py:17
  243.9 0.7 fusion.42
  244.5 41.4 %psum.91 = f32[]{:T(128)} all-reduce(f32[]{:T(128)} %fusion.42), channel_id=1, replica_groups=mesh['term'=4,'sector'=8] {'term','sector'}, use_global_device_ids=true, to_apply=%region_13.0 | all-reduce | flops 1 | bytes 8 | tf_op jit(solution)/shard_map/psum | solution.py:22
  286.9 1.2 fusion.6
  288.1 43.1 %all-reduce.11.cloned.1.call-done = bf16[8,128,128]{1,2,0:T(8,128)(2,1)} async-done(((bf16[8,128,128]{1,2,0:T(8,128)(2,1)}), bf16[8,128,128]{1,2,0:T(8,128)(2,1)}) %all-reduce.11.cloned.1.call-update) | async-done | bytes 262160 | tf_op jit(solution)/shard_map/psum | solution.py:51
  331.2 1.1 and_select_fusion
  333.0 39.6 %all-reduce = (f32[]{:T(128)}, f32[]{:T(128)}) all-reduce(f32[]{:T(128)} %get-tuple-element.5, f32[]{:T(128)} %get-tuple-element.4), channel_id=1, replica_groups=mesh['term'=4,'sector'=8] {'term','sector'}, use_global_device_ids=true, to_apply=%region_16.0 | all-reduce | flops 2 | bytes 16 | tf_op jit(solution)/shard_map/psum | solution.py:17
  373.9 0.7 fusion.41
  374.5 41.4 %psum.95 = f32[]{:T(128)} all-reduce(f32[]{:T(128)} %fusion.41), channel_id=1, replica_groups=mesh['term'=4,'sector'=8] {'term','sector'}, use_global_device_ids=true, to_apply=%region_20.0 | all-reduce | flops 1 | bytes 8 | tf_op jit(solution)/shard_map/psum | solution.py:22
  416.9 0.9 copy.9
  (28 shorter events, 3.3 us)
Async XLA Ops:
  7.2 18.6 %copy-start = (bf16[2,1,128,128]{3,2,1,0:T(8,128)(2,1)S(1)}, bf16[2,1,128,128]{3,2,1,0:T(8,128)(2,1)}, u32[]{:S(2)}) copy-start(bf16[2,1,128,128]{3,2,1,0:T(8,128)(2,1)} %param.6) | copy-start | bytes 196612
  7.2 64.0 %all-reduce.7.cloned.1.call-start = ((), (), s32[]{:S(2)}) async-start(), calls=%async_computation | async-start | bytes 524288 | tf_op jit(solution)/shard_map/psum | solution.py:51
  7.2 0.7 copy-start.6
  8.0 1.2 copy-start.5
  27.0 0.9 copy-start.4
  27.0 174.2 %all-reduce.9.cloned.1.call-start = ((), (), s32[]{:S(2)}) async-start(), calls=%async_computation.1 | async-start | bytes 524288 | tf_op jit(solution)/shard_map/psum | solution.py:51
  72.9 83.6 %copy-start.1 = (bf16[8,128,128]{1,2,0:T(8,128)(2,1)S(1)}, bf16[8,128,128]{1,2,0:T(8,128)(2,1)}, u32[]{:S(2)}) copy-start(bf16[8,128,128]{1,2,0:T(8,128)(2,1)} %all-reduce.7.cloned.1.call-done) | copy-start | bytes 786436
  158.1 173.1 %all-reduce.11.cloned.1.call-start = ((), (), s32[]{:S(2)}) async-start(), calls=%async_computation.2 | async-start | bytes 524288 | tf_op jit(solution)/shard_map/psum | solution.py:51
  203.0 83.6 %copy-start.3 = (bf16[8,128,128]{1,2,0:T(8,128)(2,1)S(1)}, bf16[8,128,128]{1,2,0:T(8,128)(2,1)}, u32[]{:S(2)}) copy-start(bf16[8,128,128]{1,2,0:T(8,128)(2,1)} %all-reduce.9.cloned.1.call-done) | copy-start | bytes 786436
  333.0 83.6 %copy-start.2 = (bf16[8,128,128]{1,2,0:T(8,128)(2,1)S(1)}, bf16[8,128,128]{1,2,0:T(8,128)(2,1)}, u32[]{:S(2)}) copy-start(bf16[8,128,128]{1,2,0:T(8,128)(2,1)} %all-reduce.11.cloned.1.call-done) | copy-start | bytes 786436
Sparse Core Ops, SparseCore 0:
  27.1 43.9 all-reduce.6
  158.2 42.9 all-reduce.8
  288.2 42.9 all-reduce.10
where the time goes:
time: 426 us; the launch traced here: 425 us
  blocking collectives  259 us (61%)
  waiting for transfers between devices  129 us (30%)
  between operations  20 us (5%)
  other arithmetic  8.96 us (2%)
    psum x3, waiting for transfers between devices, local(): lax.psum(partial_value.astype(jnp.bfloat16), 'term').astype(jnp.float32)  129 us
    psum x3, blocking collectives, dot_sums(): squares = lax.psum(jnp.sum(fresh * fresh), ('term', 'sector'))  124 us
    psum x3, blocking collectives, dot_sums(): lax.psum((jnp.sum(cur_share * cur_share), jnp.sum(cur_share * img_share))...  119 us
    all_gather x1, blocking collectives, local(): right_all = lax.all_gather(right_env, 'sector', axis=1, tiled=True)  16.6 us
  transfers between devices with their start and end apart: 3, of which 3 were waited for; matrix products, arithmetic and copies ran while one was open for 0% of the time, Pallas kernels for 0%

commit v1 on v0

--- a/solution.py
+++ b/solution.py
@@ -38,7 +38,24 @@
     def portion(values):
         return lax.dynamic_slice_in_dim(values, share_start, share, 0)
 
-    right_all = lax.all_gather(right_env, "sector", axis=1, tiled=True)
+    ways, here, k = (lax.axis_size("sector"), lax.axis_index("sector"), right_env.shape[1])
+    shape = [n * ways if d == 1 else n for d, n in enumerate(right_env.shape)]
+    right_all = lax.dynamic_update_slice_in_dim(
+        jnp.zeros(shape, right_env.dtype), right_env, here * k, axis=1
+    )
+    going_up = going_down = right_env
+    for far in range(1, ways // 2 + 1):
+        going_up = lax.ppermute(going_up, "sector", [(d, (d + 1) % ways) for d in range(ways)])
+        right_all = lax.dynamic_update_slice_in_dim(
+            right_all, going_up, (here - far) % ways * k, axis=1
+        )
+        if 2 * far < ways:
+            going_down = lax.ppermute(
+                going_down, "sector", [(d, (d - 1) % ways) for d in range(ways)]
+            )
+            right_all = lax.dynamic_update_slice_in_dim(
+                right_all, going_down, (here + far) % ways * k, axis=1
+            )
     energies = []
     for step in range(ITERS):
         images = jnp.einsum(

time: 426 us -> 433 us (1.016)
  blocking collectives: 259 us -> 243 us
  starting transfers between devices: 0.12 us -> 12 us
  waiting for transfers between devices: 129 us -> 139 us
    all_gather x1 -> x0, blocking collectives: 16.6 us -> none  [local(): right_all = lax.all_gather(right_env, 'sector', axis=1, tiled=True)]
    ppermute x0 -> x7, waiting for transfers between devices: none -> 12.8 us  [the longest x4 10.9 us: local(): lax.ppermute(going_up, 'sector', [(d, (d + 1) % ways) for d in range(ways)])]
    ppermute x0 -> x7, starting transfers between devices: none -> 11.8 us  [the longest x3 11.8 us: local(): lax.ppermute(going_down, 'sector', [(d, (d - 1) % ways) for d in range(wa...]
  transfers between devices with their start and end apart: 3 -> 10, of which waited for: 3 -> 6; matrix products, arithmetic and copies ran while one was open for 0% -> 0% of each run, Pallas kernels for 0% -> 0%
where the time goes in v1:
time: 433 us; the launch traced here: 431 us
  blocking collectives  243 us (56%)
  waiting for transfers between devices  139 us (32%)
  between operations  20.1 us (5%)
  starting transfers between devices  12 us (3%)
  other arithmetic  8.96 us (2%)
  local copies, waits for them, and re-layouts  4.65 us (1%)
    psum x3, waiting for transfers between devices, local(): lax.psum(partial_value.astype(jnp.bfloat16), 'term').astype(jnp.float32)  126 us
    psum x3, blocking collectives, dot_sums(): squares = lax.psum(jnp.sum(fresh * fresh), ('term', 'sector'))  124 us
    psum x3, blocking collectives, dot_sums(): lax.psum((jnp.sum(cur_share * cur_share), jnp.sum(cur_share * img_share))...  119 us
    ppermute x3, starting transfers between devices, local(): lax.ppermute(going_down, 'sector', [(d, (d - 1) % ways) for d in range(wa...  11.8 us
    ppermute x4, waiting for transfers between devices, local(): lax.ppermute(going_up, 'sector', [(d, (d + 1) % ways) for d in range(ways)])  10.9 us
  transfers between devices with their start and end apart: 10, of which 6 were waited for; matrix products, arithmetic and copies ran while one was open for 0% of the time, Pallas kernels for 0%

profile of v1, /device:TPU:0, one launch (start us, length us, event | category | flops | bytes accessed | tf_op | source)
XLA Modules:
  0.0 431.2 jit_solution(1075891830632880875)
XLA Ops:
  7.2 4.5 %collective-permute-start.1 = (bf16[2,1,128,128]{3,2,1,0:T(8,128)(2,1)}, bf16[2,1,128,128]{3,2,1,0:T(8,128)(2,1)S(1)}, u32[]{:S(2)}, u32[]{:S(2)}) collective-permute-start(bf16[2,1,128,128]{3,2,1,0:T(8,128)(2,1)} %param.7), channel_id=1, source_target_pairs={{0,7},{1,0},{2,1},{3,2},{4,3},{5,4},{6,5},{7,6},{8,15},{9,8},{10,9... | collective-permute-start | bytes 196616 | tf_op jit(solution)/shard_map/ppermute | solution.py:53
  12.5 1.1 copy.7
  14.5 3.6 collective-permute-start.3
  18.2 1.9 collective-permute-done.3
  20.0 3.7 collective-permute-start.5
  23.8 5.4 %collective-permute-done.4 = bf16[2,1,128,128]{3,2,1,0:T(8,128)(2,1)S(1)} collective-permute-done((bf16[2,1,128,128]{3,2,1,0:T(8,128)(2,1)S(1)}, bf16[2,1,128,128]{3,2,1,0:T(8,128)(2,1)S(1)}, u32[]{:S(2)}, u32[]{:S(2)}) %collective-permute-start.4) | collective-permute-done | bytes 65568 | tf_op jit(solution)/shard_map/ppermute | solution.py:48
  29.3 5.4 %collective-permute-done.6 = bf16[2,1,128,128]{3,2,1,0:T(8,128)(2,1)S(1)} collective-permute-done((bf16[2,1,128,128]{3,2,1,0:T(8,128)(2,1)S(1)}, bf16[2,1,128,128]{3,2,1,0:T(8,128)(2,1)S(1)}, u32[]{:S(2)}, u32[]{:S(2)}) %collective-permute-start.6) | collective-permute-done | bytes 65568 | tf_op jit(solution)/shard_map/ppermute | solution.py:48
  34.8 1.3 fusion.8
  36.1 0.9 copy-done.4
  37.2 40.1 %all-reduce.7.cloned.1.call-done = bf16[8,128,128]{1,2,0:T(8,128)(2,1)} async-done(((bf16[8,128,128]{1,2,0:T(8,128)(2,1)}), bf16[8,128,128]{1,2,0:T(8,128)(2,1)}) %all-reduce.7.cloned.1.call-update) | async-done | bytes 262160 | tf_op jit(solution)/shard_map/psum | solution.py:68
  77.4 1.2 fusion.34
  79.2 39.6 %all-reduce.2 = (f32[]{:T(128)}, f32[]{:T(128)}) all-reduce(f32[]{:T(128)} %get-tuple-element.9, f32[]{:T(128)} %get-tuple-element.8), channel_id=1, replica_groups=mesh['term'=4,'sector'=8] {'term','sector'}, use_global_device_ids=true, to_apply=%region_2.3 | all-reduce | flops 2 | bytes 16 | tf_op jit(solution)/shard_map/psum | solution.py:17
  120.8 41.4 %psum.87 = f32[]{:T(128)} all-reduce(f32[]{:T(128)} %fusion.43), channel_id=1, replica_groups=mesh['term'=4,'sector'=8] {'term','sector'}, use_global_device_ids=true, to_apply=%region_6.7 | all-reduce | flops 1 | bytes 8 | tf_op jit(solution)/shard_map/psum | solution.py:22
  163.1 1.2 fusion.7
  164.4 43.0 %all-reduce.9.cloned.1.call-done = bf16[8,128,128]{1,2,0:T(8,128)(2,1)} async-done(((bf16[8,128,128]{1,2,0:T(8,128)(2,1)}), bf16[8,128,128]{1,2,0:T(8,128)(2,1)}) %all-reduce.9.cloned.1.call-update) | async-done | bytes 262160 | tf_op jit(solution)/shard_map/psum | solution.py:68
  207.4 1.1 and_select_fusion.1
  209.2 39.6 %all-reduce.1 = (f32[]{:T(128)}, f32[]{:T(128)}) all-reduce(f32[]{:T(128)} %get-tuple-element.7, f32[]{:T(128)} %get-tuple-element.6), channel_id=1, replica_groups=mesh['term'=4,'sector'=8] {'term','sector'}, use_global_device_ids=true, to_apply=%region_9.10 | all-reduce | flops 2 | bytes 16 | tf_op jit(solution)/shard_map/psum | solution.py:17
  250.8 41.4 %psum.91 = f32[]{:T(128)} all-reduce(f32[]{:T(128)} %fusion.42), channel_id=1, replica_groups=mesh['term'=4,'sector'=8] {'term','sector'}, use_global_device_ids=true, to_apply=%region_13.14 | all-reduce | flops 1 | bytes 8 | tf_op jit(solution)/shard_map/psum | solution.py:22
  293.2 1.2 fusion.6
  294.4 43.1 %all-reduce.11.cloned.1.call-done = bf16[8,128,128]{1,2,0:T(8,128)(2,1)} async-done(((bf16[8,128,128]{1,2,0:T(8,128)(2,1)}), bf16[8,128,128]{1,2,0:T(8,128)(2,1)}) %all-reduce.11.cloned.1.call-update) | async-done | bytes 262160 | tf_op jit(solution)/shard_map/psum | solution.py:68
  337.5 1.1 and_select_fusion
  339.3 39.6 %all-reduce = (f32[]{:T(128)}, f32[]{:T(128)}) all-reduce(f32[]{:T(128)} %get-tuple-element.5, f32[]{:T(128)} %get-tuple-element.4), channel_id=1, replica_groups=mesh['term'=4,'sector'=8] {'term','sector'}, use_global_device_ids=true, to_apply=%region_16.17 | all-reduce | flops 2 | bytes 16 | tf_op jit(solution)/shard_map/psum | solution.py:17
  380.9 41.4 %psum.95 = f32[]{:T(128)} all-reduce(f32[]{:T(128)} %fusion.41), channel_id=1, replica_groups=mesh['term'=4,'sector'=8] {'term','sector'}, use_global_device_ids=true, to_apply=%region_20.21 | all-reduce | flops 1 | bytes 8 | tf_op jit(solution)/shard_map/psum | solution.py:22
  423.2 0.9 copy.9
  (50 shorter events, 7.5 us)
Async XLA Ops:
  7.2 27.6 %copy-start = (bf16[2,1,128,128]{3,2,1,0:T(8,128)(2,1)S(1)}, bf16[2,1,128,128]{3,2,1,0:T(8,128)(2,1)}, u32[]{:S(2)}) copy-start(bf16[2,1,128,128]{3,2,1,0:T(8,128)(2,1)} %param.6) | copy-start | bytes 196612
  7.2 70.2 %all-reduce.7.cloned.1.call-start = ((), (), s32[]{:S(2)}) async-start(), calls=%async_computation | async-start | bytes 524288 | tf_op jit(solution)/shard_map/psum | solution.py:68
  7.2 7.3 %collective-permute-start.1 = (bf16[2,1,128,128]{3,2,1,0:T(8,128)(2,1)}, bf16[2,1,128,128]{3,2,1,0:T(8,128)(2,1)S(1)}, u32[]{:S(2)}, u32[]{:S(2)}) collective-permute-start(bf16[2,1,128,128]{3,2,1,0:T(8,128)(2,1)} %param.7), channel_id=1, source_target_pairs={{0,7},{1,0},{2,1},{3,2},{4,3},{5,4},{6,5},{7,6},{8,15},{9,8},{10,9... | collective-permute-start | bytes 196616 | tf_op jit(solution)/shard_map/ppermute | solution.py:53
  11.8 6.4 %collective-permute-start = (bf16[2,1,128,128]{3,2,1,0:T(8,128)(2,1)}, bf16[2,1,128,128]{3,2,1,0:T(8,128)(2,1)S(1)}, u32[]{:S(2)}, u32[]{:S(2)}) collective-permute-start(bf16[2,1,128,128]{3,2,1,0:T(8,128)(2,1)} %param.7), channel_id=1, source_target_pairs={{0,1},{1,2},{2,3},{3,4},{4,5},{5,6},{6,7},{7,0},{8,9},{9,10},{10,1... | collective-permute-start | bytes 196616 | tf_op jit(solution)/shard_map/ppermute | solution.py:48
  11.8 0.7 copy-start.6
  13.7 0.8 copy-start.5
  14.5 5.5 %collective-permute-start.3 = (bf16[2,1,128,128]{3,2,1,0:T(8,128)(2,1)S(1)}, bf16[2,1,128,128]{3,2,1,0:T(8,128)(2,1)S(1)}, u32[]{:S(2)}, u32[]{:S(2)}) collective-permute-start(bf16[2,1,128,128]{3,2,1,0:T(8,128)(2,1)S(1)} %collective-permute-done.1), channel_id=1, source_target_pairs={{0,7},{1,0},{2,1},{3,2},{4,3},{5,4},{6,5},{7,6},{8,15},{9,8},{10,9... | collective-permute-start | bytes 196616 | tf_op jit(solution)/shard_map/ppermute | solution.py:53
  18.1 5.6 %collective-permute-start.2 = (bf16[2,1,128,128]{3,2,1,0:T(8,128)(2,1)S(1)}, bf16[2,1,128,128]{3,2,1,0:T(8,128)(2,1)S(1)}, u32[]{:S(2)}, u32[]{:S(2)}) collective-permute-start(bf16[2,1,128,128]{3,2,1,0:T(8,128)(2,1)S(1)} %collective-permute-done), channel_id=1, source_target_pairs={{0,1},{1,2},{2,3},{3,4},{4,5},{5,6},{6,7},{7,0},{8,9},{9,10},{10,1... | collective-permute-start | bytes 196616 | tf_op jit(solution)/shard_map/ppermute | solution.py:48
  20.0 9.2 %collective-permute-start.5 = (bf16[2,1,128,128]{3,2,1,0:T(8,128)(2,1)S(1)}, bf16[2,1,128,128]{3,2,1,0:T(8,128)(2,1)S(1)}, u32[]{:S(2)}, u32[]{:S(2)}) collective-permute-start(bf16[2,1,128,128]{3,2,1,0:T(8,128)(2,1)S(1)} %collective-permute-done.3), channel_id=1, source_target_pairs={{0,7},{1,0},{2,1},{3,2},{4,3},{5,4},{6,5},{7,6},{8,15},{9,8},{10,9... | collective-permute-start | bytes 196616 | tf_op jit(solution)/shard_map/ppermute | solution.py:53
  23.8 5.5 %collective-permute-start.4 = (bf16[2,1,128,128]{3,2,1,0:T(8,128)(2,1)S(1)}, bf16[2,1,128,128]{3,2,1,0:T(8,128)(2,1)S(1)}, u32[]{:S(2)}, u32[]{:S(2)}) collective-permute-start(bf16[2,1,128,128]{3,2,1,0:T(8,128)(2,1)S(1)} %collective-permute-done.2), channel_id=1, source_target_pairs={{0,1},{1,2},{2,3},{3,4},{4,5},{5,6},{6,7},{7,0},{8,9},{9,10},{10,1... | collective-permute-start | bytes 196616 | tf_op jit(solution)/shard_map/ppermute | solution.py:48
  29.3 5.5 %collective-permute-start.6 = (bf16[2,1,128,128]{3,2,1,0:T(8,128)(2,1)S(1)}, bf16[2,1,128,128]{3,2,1,0:T(8,128)(2,1)S(1)}, u32[]{:S(2)}, u32[]{:S(2)}) collective-permute-start(bf16[2,1,128,128]{3,2,1,0:T(8,128)(2,1)S(1)} %collective-permute-done.4), channel_id=1, source_target_pairs={{0,1},{1,2},{2,3},{3,4},{4,5},{5,6},{6,7},{7,0},{8,9},{9,10},{10,1... | collective-permute-start | bytes 196616 | tf_op jit(solution)/shard_map/ppermute | solution.py:48
  36.1 0.9 copy-start.4
  36.1 171.3 %all-reduce.9.cloned.1.call-start = ((), (), s32[]{:S(2)}) async-start(), calls=%async_computation.1 | async-start | bytes 524288 | tf_op jit(solution)/shard_map/psum | solution.py:68
  79.2 83.6 %copy-start.1 = (bf16[8,128,128]{1,2,0:T(8,128)(2,1)S(1)}, bf16[8,128,128]{1,2,0:T(8,128)(2,1)}, u32[]{:S(2)}) copy-start(bf16[8,128,128]{1,2,0:T(8,128)(2,1)} %all-reduce.7.cloned.1.call-done) | copy-start | bytes 786436
  164.3 173.1 %all-reduce.11.cloned.1.call-start = ((), (), s32[]{:S(2)}) async-start(), calls=%async_computation.2 | async-start | bytes 524288 | tf_op jit(solution)/shard_map/psum | solution.py:68
  209.2 83.6 %copy-start.3 = (bf16[8,128,128]{1,2,0:T(8,128)(2,1)S(1)}, bf16[8,128,128]{1,2,0:T(8,128)(2,1)}, u32[]{:S(2)}) copy-start(bf16[8,128,128]{1,2,0:T(8,128)(2,1)} %all-reduce.9.cloned.1.call-done) | copy-start | bytes 786436
  339.3 83.6 %copy-start.2 = (bf16[8,128,128]{1,2,0:T(8,128)(2,1)S(1)}, bf16[8,128,128]{1,2,0:T(8,128)(2,1)}, u32[]{:S(2)}) copy-start(bf16[8,128,128]{1,2,0:T(8,128)(2,1)} %all-reduce.11.cloned.1.call-done) | copy-start | bytes 786436
Sparse Core Ops, SparseCore 0:
  36.2 41.1 all-reduce.6
  164.5 42.9 all-reduce.8
  294.5 42.9 all-reduce.10
